TPU v7x, 128 devices: a whole 4x4x4 slice. The times are simulated.
128 devices in a mesh: gx: 16 (over x, z_hi, core), gy: 8 (over z_lo, y).
Axes of the slice: x: 4, y: 4, z: 4 (z_hi: 2, z_lo: 2; z = z_hi * 2 + z_lo), core: 2. Of those that a mesh axis runs over, the one named last changes fastest.
Arguments:
- volume: bfloat16 [64, 32, 128, 128], P(None, 'gx', 'gy'), may hold values from -6 to 6
- kernel: bfloat16 [4, 4, 4, 32, 64], replicated, may hold values from -0.25 to 0.25
- cotangent: bfloat16 [2, 2, 2, 32, 32, 128, 128], P(None, None, None, None, 'gx', 'gy'), may hold values from -6 to 6
Outputs:
- activation: bfloat16 [2, 2, 2, 32, 32, 128, 128], P(None, None, None, None, 'gx', 'gy')
- input_grad: bfloat16 [64, 32, 128, 128], P(None, 'gx', 'gy')
- weight_grad: float32 [4, 4, 4, 32, 64], replicated
All inputs are finite; a program needn't handle non-finite values.
Results may differ from a plain program's by a relative error of at most 0.0049.
Values may be sent and summed in bfloat16 or wider, within the bound.
A program may use at most 192 MiB of HBM per device.

v0:
```python
import math
import jax
import jax.numpy as jnp
from jax import lax
from jax.sharding import PartitionSpec as P

FORWARD_TAPS = (((1, 0), (3, -1)), ((2, 0), (0, 1)))
PHASE_TAPS = (((1, 0), (3, 1)), ((0, -1), (2, 0)))


def padded_2(block, sides, width):
    for axis, dim in sides:
        count = lax.axis_size(axis)
        forward = [(i, i + 1) for i in range(count - 1)]
        backward = [(target, source) for source, target in forward]
        low = lax.ppermute(
            lax.slice_in_dim(block, block.shape[dim] - width, None, axis=dim), axis, forward
        )
        high = lax.ppermute(lax.slice_in_dim(block, 0, width, axis=dim), axis, backward)
        block = jnp.concatenate([low, block, high], axis=dim)
    return block


def silu_pair(before):
    sigmoid = jax.nn.sigmoid(before)
    return (before * sigmoid, sigmoid * (1.0 + before * (1.0 - sigmoid)))


def phase_product(padded, kernel, phase_x, phase_y, phase_z, span_x, span_y, depth_cells):
    total = None
    for tap_x, shift_x in FORWARD_TAPS[phase_x]:
        for tap_y, shift_y in FORWARD_TAPS[phase_y]:
            for tap_z, shift_z in FORWARD_TAPS[phase_z]:
                piece = lax.slice(
                    padded,
                    (0, 1 + shift_x, 1 + shift_y, 1 + shift_z),
                    (
                        padded.shape[0],
                        1 + shift_x + span_x,
                        1 + shift_y + span_y,
                        1 + shift_z + depth_cells,
                    ),
                )
                term = lax.dot_general(
                    kernel[tap_x, tap_y, tap_z],
                    piece,
                    (((1,), (0,)), ((), ())),
                    preferred_element_type=jnp.float32,
                )
                total = term if total is None else total + term
    return total


def all_phases(padded, kernel, span_x, span_y, depth_cells):
    results = []
    for phase_x in range(2):
        for phase_y in range(2):
            for phase_z in range(2):
                results.append(
                    phase_product(
                        padded, kernel, phase_x, phase_y, phase_z, span_x, span_y, depth_cells
                    )
                )
    chans_out = results[0].shape[0]
    return jnp.stack(results).reshape(2, 2, 2, chans_out, span_x, span_y, depth_cells)


def on_device(volume, kernel, cotangent):
    cells_x = volume.shape[1]
    cells_y = volume.shape[2]
    depth_cells = volume.shape[3]
    rim_cells = padded_2(volume, (("gx", 1), ("gy", 2)), 1)
    padded = jnp.pad(rim_cells, ((0, 0), (0, 0), (0, 0), (1, 1)))
    before = all_phases(padded, kernel, cells_x, cells_y, depth_cells)
    values, slopes = silu_pair(before)
    activation = values.astype(jnp.bfloat16)
    grad_pre = (cotangent.astype(jnp.float32) * slopes).astype(jnp.bfloat16)
    grad_rim = padded_2(grad_pre, (("gx", 4), ("gy", 5)), 1)
    grad_pad = jnp.pad(grad_rim, ((0, 0), (0, 0), (0, 0), (0, 0), (0, 0), (0, 0), (1, 1)))
    chans_out = grad_pad.shape[3]
    back_sum = None
    weight_parts = [None] * 64
    for phase_x in range(2):
        for phase_y in range(2):
            for phase_z in range(2):
                source = grad_pad[phase_x, phase_y, phase_z]
                group_list = []
                group_slots = []
                for tap_x, shift_x in PHASE_TAPS[phase_x]:
                    for tap_y, shift_y in PHASE_TAPS[phase_y]:
                        for tap_z, shift_z in PHASE_TAPS[phase_z]:
                            piece = lax.slice(
                                source,
                                (0, 1 + shift_x, 1 + shift_y, 1 + shift_z),
                                (
                                    chans_out,
                                    1 + shift_x + cells_x,
                                    1 + shift_y + cells_y,
                                    1 + shift_z + depth_cells,
                                ),
                            )
                            product = lax.dot_general(
                                kernel[tap_x, tap_y, tap_z],
                                piece,
                                (((0,), (0,)), ((), ())),
                                preferred_element_type=jnp.float32,
                            )
                            back_sum = product if back_sum is None else back_sum + product
                            group_list.append(
                                lax.dot_general(
                                    piece,
                                    volume,
                                    (((1, 2, 3), (1, 2, 3)), ((), ())),
                                    preferred_element_type=jnp.float32,
                                )
                            )
                            group_slots.append(16 * tap_x + 4 * tap_y + tap_z)
                group_terms = jnp.stack(group_list)
                for position, flat_index in enumerate(group_slots):
                    weight_parts[flat_index] = group_terms[position]
    input_grad = back_sum.astype(jnp.bfloat16)
    stacked_grad = jnp.stack(weight_parts).reshape(4, 4, 4, chans_out, volume.shape[0])
    stacked_grad = lax.psum(stacked_grad, ("gx", "gy"))
    scaling = 1.0 / math.sqrt(
        cells_x * lax.axis_size("gx") * cells_y * lax.axis_size("gy") * depth_cells
    )
    return (activation, input_grad, stacked_grad * scaling)


def solution(mesh):
    placed = (P(None, "gx", "gy", None), P(), P(None, None, None, None, "gx", "gy", None))
    return jax.shard_map(
        on_device,
        mesh=mesh,
        in_specs=placed,
        out_specs=(P(None, None, None, None, "gx", "gy", None), P(None, "gx", "gy", None), P()),
        check_vma=False,
    )
```

profile of v0, /device:TPU:1, one launch (start us, length us, event | category | flops | bytes accessed | tf_op | source)
XLA Modules:
  0.0 342.6 jit_solution(13506336892047364948)
XLA Ops:
  8.6 6.9 %collective-permute-start = (bf16[64,1,16,128]{3,0,2,1:T(8,128)(2,1)S(1)}, bf16[64,1,16,128]{3,0,2,1:T(8,128)(2,1)S(1)}, u32[]{:S(2)}, u32[]{:S(2)}) collective-permute-start(bf16[64,1,16,128]{3,0,2,1:T(8,128)(2,1)S(1)} %get-tuple-element.25), channel_id=1, source_target_pairs={{0,8},{8,16},{16,24},{24,32},{32,40},{40,48},{48,56},{56,64},{64,7... | collective-permute-start | bytes 786440 | tf_op jit(solution)/shard_map/ppermute | solution.py:16
  15.5 1.9 collective-permute-start.1
  20.0 4.7 %collective-permute-done.1 = bf16[64,1,16,128]{3,0,2,1:T(8,128)(2,1)S(1)} collective-permute-done((bf16[64,1,16,128]{3,0,2,1:T(8,128)(2,1)S(1)}, bf16[64,1,16,128]{3,0,2,1:T(8,128)(2,1)S(1)}, u32[]{:S(2)}, u32[]{:S(2)}) %collective-permute-start.1) | collective-permute-done | bytes 262176 | tf_op jit(solution)/shard_map/ppermute | solution.py:19
  24.7 3.2 collective-permute-start.2
  31.0 2.0 collective-permute-done.3
  33.0 1.8 fusion.11
  49.2 2.5 multiply_convert_fusion
  52.1 3.4 collective-permute-start.4
  55.5 1.9 collective-permute-start.5
  57.4 23.8 %collective-permute-done.4 = bf16[2,2,2,32,1,16,128]{6,3,5,4,2,1,0:T(8,128)(2,1)S(1)} collective-permute-done((bf16[2,2,2,32,1,16,128]{6,3,5,4,2,1,0:T(8,128)(2,1)S(1)}, bf16[2,2,2,32,1,16,128]{6,3,5,4,2,1,0:T(8,128)(2,1)S(1)}, u32[]{:S(2)}, u32[]{:S(2)}) %collective-permute-start.4) | collective-permute-done | bytes 1048608 | tf_op jit(solution)/shard_map/ppermute | solution.py:16
  83.9 2.1 copy.84
  86.1 3.7 %collective-permute-done.7 = bf16[2,2,2,32,4,1,128]{6,3,5,4,2,1,0:T(8,128)(2,1)S(1)} collective-permute-done((bf16[2,2,2,32,4,1,128]{6,3,5,4,2,1,0:T(8,128)(2,1)S(1)}, bf16[2,2,2,32,4,1,128]{6,3,5,4,2,1,0:T(8,128)(2,1)S(1)}, u32[]{:S(2)}, u32[]{:S(2)}) %collective-permute-start.7) | collective-permute-done | bytes 262176 | tf_op jit(solution)/shard_map/ppermute | solution.py:19
  89.8 8.8 %select_maximum_fusion = bf16[2,2,2,32,4,18,130]{6,3,5,4,2,1,0:T(8,128)(2,1)S(1)} fusion(bf16[2,2,2,32,4,1,128]{6,3,5,4,2,1,0:T(8,128)(2,1)S(1)} %collective-permute-done.7, bf16[2,2,2,32,4,1,128]{6,3,5,4,2,1,0:T(8,128)(2,1)S(1)} %collective-permute-done.6, bf16[2,2,2,32,1,16,128]{6,3,5,4,2,1,0:T(8,128)(2,1)S(1)} %collective-permute-done.5, ...), kind=kLoop, calls=%fused_computation.3 | loop fusion | flops 43130880 | bytes 9510912 | tf_op jit(solution)/shard_map/concatenate | solution.py:20
  99.8 1.7 convolution_bitcast_fusion.40
  101.6 1.8 convolution_bitcast_fusion.41
  151.0 1.5 convolution_bitcast_fusion.2
  180.1 1.9 convolution_add_fusion.15
  188.2 1.8 fusion.54
  190.5 1.9 fusion.59
  193.9 1.9 fusion.58
  197.2 1.9 fusion.57
  200.4 1.9 fusion.56
  208.4 124.8 %all-reduce.4.cloned.1.call-done = f32[4,4,4,32,64]{4,3,2,1,0:T(8,128)} async-done(((f32[4,4,4,32,64]{4,3,2,1,0:T(8,128)}), f32[4,4,4,32,64]{4,3,2,1,0:T(8,128)}) %all-reduce.4.cloned.1.call-update) | async-done | bytes 524304 | tf_op jit(solution)/shard_map/psum | solution.py:123
  333.2 2.3 broadcast_multiply_fusion
  (309 shorter events, 117.2 us)
Async XLA Ops:
  7.2 10.3 %copy-start = (bf16[64,2,16,128]{3,2,1,0:T(8,128)(2,1)S(1)}, bf16[64,2,16,128]{3,2,1,0:T(8,128)(2,1)}, u32[]{:S(2)}) copy-start(bf16[64,2,16,128]{3,2,1,0:T(8,128)(2,1)} %param.3) | copy-start | bytes 1572868
  7.2 10.3 %copy-start.51 = (bf16[4,4,4,32,64]{4,3,2,1,0:T(8,128)(2,1)S(1)}, bf16[4,4,4,32,64]{4,3,2,1,0:T(8,128)(2,1)}, u32[]{:S(2)}) copy-start(bf16[4,4,4,32,64]{4,3,2,1,0:T(8,128)(2,1)} %param.4) | copy-start | bytes 786436
  7.2 326.0 %all-reduce.4.cloned.1.call-start = ((), (), s32[]{:S(2)}) async-start(), calls=%async_computation | async-start | bytes 2097152 | tf_op jit(solution)/shard_map/psum | solution.py:123
  8.6 11.1 %collective-permute-start = (bf16[64,1,16,128]{3,0,2,1:T(8,128)(2,1)S(1)}, bf16[64,1,16,128]{3,0,2,1:T(8,128)(2,1)S(1)}, u32[]{:S(2)}, u32[]{:S(2)}) collective-permute-start(bf16[64,1,16,128]{3,0,2,1:T(8,128)(2,1)S(1)} %get-tuple-element.25), channel_id=1, source_target_pairs={{0,8},{8,16},{16,24},{24,32},{32,40},{40,48},{48,56},{56,64},{64,7... | collective-permute-start | bytes 786440 | tf_op jit(solution)/shard_map/ppermute | solution.py:16
  15.5 9.2 %collective-permute-start.1 = (bf16[64,1,16,128]{3,0,2,1:T(8,128)(2,1)S(1)}, bf16[64,1,16,128]{3,0,2,1:T(8,128)(2,1)S(1)}, u32[]{:S(2)}, u32[]{:S(2)}) collective-permute-start(bf16[64,1,16,128]{3,0,2,1:T(8,128)(2,1)S(1)} %get-tuple-element.24), channel_id=1, source_target_pairs={{8,0},{16,8},{24,16},{32,24},{40,32},{48,40},{56,48},{64,56},{72,6... | collective-permute-start | bytes 786440 | tf_op jit(solution)/shard_map/ppermute | solution.py:19
  24.7 6.2 %collective-permute-start.2 = (bf16[64,4,1,128]{3,0,2,1:T(8,128)(2,1)S(1)}, bf16[64,4,1,128]{3,0,2,1:T(8,128)(2,1)S(1)}, u32[]{:S(2)}, u32[]{:S(2)}) collective-permute-start(bf16[64,4,1,128]{3,0,2,1:T(8,128)(2,1)S(1)} %get-tuple-element.22), channel_id=1, source_target_pairs={{0,1},{1,2},{2,3},{3,4},{4,5},{5,6},{6,7},{8,9},{9,10},{10,11},{11... | collective-permute-start | bytes 196616 | tf_op jit(solution)/shard_map/ppermute | solution.py:16
  28.0 5.0 %collective-permute-start.3 = (bf16[64,4,1,128]{3,0,2,1:T(8,128)(2,1)S(1)}, bf16[64,4,1,128]{3,0,2,1:T(8,128)(2,1)S(1)}, u32[]{:S(2)}, u32[]{:S(2)}) collective-permute-start(bf16[64,4,1,128]{3,0,2,1:T(8,128)(2,1)S(1)} %get-tuple-element.23), channel_id=1, source_target_pairs={{1,0},{2,1},{3,2},{4,3},{5,4},{6,5},{7,6},{9,8},{10,9},{11,10},{12... | collective-permute-start | bytes 196616 | tf_op jit(solution)/shard_map/ppermute | solution.py:19
  52.1 29.1 %collective-permute-start.4 = (bf16[2,2,2,32,1,16,128]{6,3,5,4,2,1,0:T(8,128)(2,1)S(1)}, bf16[2,2,2,32,1,16,128]{6,3,5,4,2,1,0:T(8,128)(2,1)S(1)}, u32[]{:S(2)}, u32[]{:S(2)}) collective-permute-start(bf16[2,2,2,32,1,16,128]{6,3,5,4,2,1,0:T(8,128)(2,1)S(1)} %get-tuple-element.18), channel_id=1, source_target_pairs={{0,8},{8,16},{16,24},{24,32},{32,40},{40,48},{48,56},{56,64},{64,7... | collective-permute-start | bytes 3145736 | tf_op jit(solution)/shard_map/ppermute | solution.py:16
  55.5 25.8 %collective-permute-start.5 = (bf16[2,2,2,32,1,16,128]{6,3,5,4,2,1,0:T(8,128)(2,1)S(1)}, bf16[2,2,2,32,1,16,128]{6,3,5,4,2,1,0:T(8,128)(2,1)S(1)}, u32[]{:S(2)}, u32[]{:S(2)}) collective-permute-start(bf16[2,2,2,32,1,16,128]{6,3,5,4,2,1,0:T(8,128)(2,1)S(1)} %get-tuple-element.19), channel_id=1, source_target_pairs={{8,0},{16,8},{24,16},{32,24},{40,32},{48,40},{56,48},{64,56},{72,6... | collective-permute-start | bytes 3145736 | tf_op jit(solution)/shard_map/ppermute | solution.py:19
  81.3 4.8 %collective-permute-start.6 = (bf16[2,2,2,32,4,1,128]{6,3,5,4,2,1,0:T(8,128)(2,1)S(1)}, bf16[2,2,2,32,4,1,128]{6,3,5,4,2,1,0:T(8,128)(2,1)S(1)}, u32[]{:S(2)}, u32[]{:S(2)}) collective-permute-start(bf16[2,2,2,32,4,1,128]{6,3,5,4,2,1,0:T(8,128)(2,1)S(1)} %get-tuple-element.14), channel_id=1, source_target_pairs={{0,1},{1,2},{2,3},{3,4},{4,5},{5,6},{6,7},{8,9},{9,10},{10,11},{11... | collective-permute-start | bytes 786440 | tf_op jit(solution)/shard_map/ppermute | solution.py:16
  82.6 7.1 %collective-permute-start.7 = (bf16[2,2,2,32,4,1,128]{6,3,5,4,2,1,0:T(8,128)(2,1)S(1)}, bf16[2,2,2,32,4,1,128]{6,3,5,4,2,1,0:T(8,128)(2,1)S(1)}, u32[]{:S(2)}, u32[]{:S(2)}) collective-permute-start(bf16[2,2,2,32,4,1,128]{6,3,5,4,2,1,0:T(8,128)(2,1)S(1)} %get-tuple-element.15), channel_id=1, source_target_pairs={{1,0},{2,1},{3,2},{4,3},{5,4},{6,5},{7,6},{9,8},{10,9},{11,10},{12... | collective-permute-start | bytes 786440 | tf_op jit(solution)/shard_map/ppermute | solution.py:19
  99.8 73.0 %copy-start.1 = (bf16[32,4,18,130]{3,0,2,1:T(8,128)(2,1)}, bf16[32,4,18,130]{3,0,2,1:T(8,128)(2,1)S(1)}, u32[]{:S(2)}) copy-start(bf16[32,4,18,130]{3,0,2,1:T(8,128)(2,1)S(1)} %get-tuple-element.8) | copy-start | bytes 1797124
  99.8 73.3 %copy-start.2 = (bf16[32,4,18,130]{3,0,2,1:T(8,128)(2,1)}, bf16[32,4,18,130]{3,0,2,1:T(8,128)(2,1)S(1)}, u32[]{:S(2)}) copy-start(bf16[32,4,18,130]{3,0,2,1:T(8,128)(2,1)S(1)} %get-tuple-element.9) | copy-start | bytes 1797124
  99.8 77.2 %copy-start.3 = (bf16[32,4,18,130]{3,0,2,1:T(8,128)(2,1)}, bf16[32,4,18,130]{3,0,2,1:T(8,128)(2,1)S(1)}, u32[]{:S(2)}) copy-start(bf16[32,4,18,130]{3,0,2,1:T(8,128)(2,1)S(1)} %get-tuple-element.10) | copy-start | bytes 1797124
  99.8 77.6 %copy-start.4 = (bf16[32,4,18,130]{3,0,2,1:T(8,128)(2,1)}, bf16[32,4,18,130]{3,0,2,1:T(8,128)(2,1)S(1)}, u32[]{:S(2)}) copy-start(bf16[32,4,18,130]{3,0,2,1:T(8,128)(2,1)S(1)} %get-tuple-element.11) | copy-start | bytes 1797124
  99.8 78.6 %copy-start.5 = (bf16[32,4,18,130]{3,0,2,1:T(8,128)(2,1)}, bf16[32,4,18,130]{3,0,2,1:T(8,128)(2,1)S(1)}, u32[]{:S(2)}) copy-start(bf16[32,4,18,130]{3,0,2,1:T(8,128)(2,1)S(1)} %get-tuple-element.6) | copy-start | bytes 1797124
  99.8 78.9 %copy-start.7 = (bf16[32,4,18,130]{3,0,2,1:T(8,128)(2,1)}, bf16[32,4,18,130]{3,0,2,1:T(8,128)(2,1)S(1)}, u32[]{:S(2)}) copy-start(bf16[32,4,18,130]{3,0,2,1:T(8,128)(2,1)S(1)} %get-tuple-element.12) | copy-start | bytes 1797124
  187.0 3.0 copy-start.49
  190.5 3.0 copy-start.41
  190.5 3.3 copy-start.42
  193.9 3.2 copy-start.35
  197.1 3.3 copy-start.28
  200.4 3.0 copy-start.20
  200.4 3.3 copy-start.21
  (38 other events, 81.7 us)
Sparse Core Ops, SparseCore 0:
  180.2 152.9 all-reduce.3
where the time goes:
time: 346 us; the launch traced here: 343 us
  waiting for transfers between devices  159 us (46%)
  matrix products  114 us (33%)
  starting transfers between devices  21.2 us (6%)
  local copies, waits for them, and re-layouts  17.6 us (5%)
  other arithmetic  15.5 us (4%)
  between operations  15.3 us (4%)
    psum x1, waiting for transfers between devices, on_device(): stacked_grad = lax.psum(stacked_grad, ('gx', 'gy'))  125 us
    dot_general x64, matrix products, on_device(): lax.dot_general(kernel[tap_x, tap_y, tap_z], piece, (((0,), (0,)), ((), (...  75.5 us
    ppermute x4, waiting for transfers between devices, padded_2(): lax.ppermute(lax.slice_in_dim(block, block.shape[dim] - width, None, axis...  23.8 us
    dot_general x64, matrix products, on_device(): lax.dot_general(piece, volume, (((1, 2, 3), (1, 2, 3)), ((), ())), prefer...  21.3 us
    dot_general x64, matrix products, phase_product(): lax.dot_general(kernel[tap_x, tap_y, tap_z], piece, (((1,), (0,)), ((), (...  17 us
    unnamed x111, local copies, waits for them, and re-layouts  15.9 us
    ppermute x4, starting transfers between devices, padded_2(): lax.ppermute(lax.slice_in_dim(block, block.shape[dim] - width, None, axis...  14.8 us
    concatenate x3, other arithmetic, padded_2(): block = jnp.concatenate([low, block, high], axis=dim)  10.7 us
  transfers between devices with their start and end apart: 9, of which 5 were waited for; matrix products, arithmetic and copies ran while one was open for 7% of the time, Pallas kernels for 0%

commit v1 on v0

--- a/solution.py
+++ b/solution.py
@@ -120,7 +120,10 @@
                     weight_parts[flat_index] = group_terms[position]
     input_grad = back_sum.astype(jnp.bfloat16)
     stacked_grad = jnp.stack(weight_parts).reshape(4, 4, 4, chans_out, volume.shape[0])
-    stacked_grad = lax.psum(stacked_grad, ("gx", "gy"))
+    panel = stacked_grad
+    for t in ("gx", "gy"):
+        panel = lax.psum(panel, t)
+    stacked_grad = panel
     scaling = 1.0 / math.sqrt(
         cells_x * lax.axis_size("gx") * cells_y * lax.axis_size("gy") * depth_cells
     )

time: 346 us -> 417 us (1.21)
  the two profiles are of different devices: /device:TPU:1 before, /device:TPU:0 now
where the time goes in v1:
time: 417 us; the launch traced here: 413 us
  waiting for transfers between devices  230 us (55%)
  matrix products  117 us (28%)
  starting transfers between devices  20.3 us (5%)
  other arithmetic  15.5 us (4%)
  local copies, waits for them, and re-layouts  15.3 us (4%)
  between operations  15.3 us (4%)
    psum x2, waiting for transfers between devices, on_device(): panel = lax.psum(panel, t)  214 us
    dot_general x64, matrix products, on_device(): lax.dot_general(kernel[tap_x, tap_y, tap_z], piece, (((0,), (0,)), ((), (...  77.8 us
    dot_general x64, matrix products, on_device(): lax.dot_general(piece, volume, (((1, 2, 3), (1, 2, 3)), ((), ())), prefer...  21.3 us
    dot_general x64, matrix products, phase_product(): lax.dot_general(kernel[tap_x, tap_y, tap_z], piece, (((1,), (0,)), ((), (...  17.5 us
    ppermute x4, starting transfers between devices, padded_2(): lax.ppermute(lax.slice_in_dim(block, block.shape[dim] - width, None, axis...  15.1 us
    ppermute x4, waiting for transfers between devices, padded_2(): lax.ppermute(lax.slice_in_dim(block, 0, width, axis=dim), axis, backward)  14.5 us
    unnamed x103, local copies, waits for them, and re-layouts  13.6 us
    concatenate x3, other arithmetic, padded_2(): block = jnp.concatenate([low, block, high], axis=dim)  10.7 us
  transfers between devices with their start and end apart: 10, of which 8 were waited for; matrix products, arithmetic and copies ran while one was open for 7% of the time, Pallas kernels for 0%

profile of v1, /device:TPU:0, one launch (start us, length us, event | category | flops | bytes accessed | tf_op | source)
XLA Modules:
  0.0 413.3 jit_solution(13001926286987998922)
XLA Ops:
  13.8 3.8 collective-permute-done.1
  17.6 3.5 collective-permute-start.2
  24.1 3.1 collective-permute-done.3
  27.3 1.8 fusion.11
  43.9 2.5 multiply_convert_fusion
  46.8 6.8 %collective-permute-start.4 = (bf16[2,2,2,32,1,16,128]{6,3,5,4,2,1,0:T(8,128)(2,1)S(1)}, bf16[2,2,2,32,1,16,128]{6,3,5,4,2,1,0:T(8,128)(2,1)S(1)}, u32[]{:S(2)}, u32[]{:S(2)}) collective-permute-start(bf16[2,2,2,32,1,16,128]{6,3,5,4,2,1,0:T(8,128)(2,1)S(1)} %get-tuple-element.18), channel_id=1, source_target_pairs={{0,8},{8,16},{16,24},{24,32},{32,40},{40,48},{48,56},{56,64},{64,7... | collective-permute-start | bytes 3145736 | tf_op jit(solution)/shard_map/ppermute | solution.py:16
  55.8 3.3 collective-permute-done.5
  59.1 3.5 collective-permute-start.6
  64.0 2.1 copy.84
  66.5 4.4 %collective-permute-done.7 = bf16[2,2,2,32,4,1,128]{6,3,5,4,2,1,0:T(8,128)(2,1)S(1)} collective-permute-done((bf16[2,2,2,32,4,1,128]{6,3,5,4,2,1,0:T(8,128)(2,1)S(1)}, bf16[2,2,2,32,4,1,128]{6,3,5,4,2,1,0:T(8,128)(2,1)S(1)}, u32[]{:S(2)}, u32[]{:S(2)}) %collective-permute-start.7) | collective-permute-done | bytes 262176 | tf_op jit(solution)/shard_map/ppermute | solution.py:19
  70.9 8.8 %select_maximum_fusion = bf16[2,2,2,32,4,18,130]{6,3,5,4,2,1,0:T(8,128)(2,1)S(1)} fusion(bf16[2,2,2,32,4,1,128]{6,3,5,4,2,1,0:T(8,128)(2,1)S(1)} %collective-permute-done.7, bf16[2,2,2,32,4,1,128]{6,3,5,4,2,1,0:T(8,128)(2,1)S(1)} %collective-permute-done.6, bf16[2,2,2,32,1,16,128]{6,3,5,4,2,1,0:T(8,128)(2,1)S(1)} %collective-permute-done.5, ...), kind=kLoop, calls=%fused_computation.3 | loop fusion | flops 43130880 | bytes 9510912 | tf_op jit(solution)/shard_map/concatenate | solution.py:20
  81.0 1.7 convolution_bitcast_fusion.40
  82.7 1.7 convolution_bitcast_fusion.41
  158.7 1.9 convolution_add_fusion.15
  166.8 1.8 fusion.54
  169.1 1.9 fusion.59
  172.4 1.9 fusion.58
  175.7 1.9 fusion.57
  178.9 1.9 fusion.56
  182.4 1.7 fusion.55
  184.1 139.0 %all-reduce.5.cloned.1.call-done = f32[4,4,4,32,64]{4,3,2,1,0:T(8,128)} async-done(((f32[4,4,4,32,64]{4,3,2,1,0:T(8,128)}), f32[4,4,4,32,64]{4,3,2,1,0:T(8,128)}) %all-reduce.5.cloned.1.call-update) | async-done | bytes 524304 | tf_op jit(solution)/shard_map/psum | solution.py:125
  324.6 2.9 fusion.60
  328.6 75.3 %all-reduce.7.cloned.1.call-done = f32[4,4,4,32,64]{4,3,2,1,0:T(8,128)} async-done(((f32[4,4,4,32,64]{4,3,2,1,0:T(8,128)}), f32[4,4,4,32,64]{4,3,2,1,0:T(8,128)}) %all-reduce.7.cloned.1.call-update) | async-done | bytes 524304 | tf_op jit(solution)/shard_map/psum | solution.py:125
  403.9 2.3 broadcast_multiply_fusion
  (304 shorter events, 118.7 us)
Async XLA Ops:
  7.2 4.1 copy-start
  7.2 4.1 copy-start.47
  7.2 315.9 %all-reduce.5.cloned.1.call-start = ((), (), s32[]{:S(2)}) async-start(), calls=%async_computation | async-start | bytes 2097152 | tf_op jit(solution)/shard_map/psum | solution.py:125
  8.6 4.9 %collective-permute-start = (bf16[64,1,16,128]{3,0,2,1:T(8,128)(2,1)S(1)}, bf16[64,1,16,128]{3,0,2,1:T(8,128)(2,1)S(1)}, u32[]{:S(2)}, u32[]{:S(2)}) collective-permute-start(bf16[64,1,16,128]{3,0,2,1:T(8,128)(2,1)S(1)} %get-tuple-element.25), channel_id=1, source_target_pairs={{0,8},{8,16},{16,24},{24,32},{32,40},{40,48},{48,56},{56,64},{64,7... | collective-permute-start | bytes 786440 | tf_op jit(solution)/shard_map/ppermute | solution.py:16
  9.9 7.6 %collective-permute-start.1 = (bf16[64,1,16,128]{3,0,2,1:T(8,128)(2,1)S(1)}, bf16[64,1,16,128]{3,0,2,1:T(8,128)(2,1)S(1)}, u32[]{:S(2)}, u32[]{:S(2)}) collective-permute-start(bf16[64,1,16,128]{3,0,2,1:T(8,128)(2,1)S(1)} %get-tuple-element.24), channel_id=1, source_target_pairs={{8,0},{16,8},{24,16},{32,24},{40,32},{48,40},{56,48},{64,56},{72,6... | collective-permute-start | bytes 786440 | tf_op jit(solution)/shard_map/ppermute | solution.py:19
  17.6 6.5 %collective-permute-start.2 = (bf16[64,4,1,128]{3,0,2,1:T(8,128)(2,1)S(1)}, bf16[64,4,1,128]{3,0,2,1:T(8,128)(2,1)S(1)}, u32[]{:S(2)}, u32[]{:S(2)}) collective-permute-start(bf16[64,4,1,128]{3,0,2,1:T(8,128)(2,1)S(1)} %get-tuple-element.22), channel_id=1, source_target_pairs={{0,1},{1,2},{2,3},{3,4},{4,5},{5,6},{6,7},{8,9},{9,10},{10,11},{11... | collective-permute-start | bytes 196616 | tf_op jit(solution)/shard_map/ppermute | solution.py:16
  21.1 6.2 %collective-permute-start.3 = (bf16[64,4,1,128]{3,0,2,1:T(8,128)(2,1)S(1)}, bf16[64,4,1,128]{3,0,2,1:T(8,128)(2,1)S(1)}, u32[]{:S(2)}, u32[]{:S(2)}) collective-permute-start(bf16[64,4,1,128]{3,0,2,1:T(8,128)(2,1)S(1)} %get-tuple-element.23), channel_id=1, source_target_pairs={{1,0},{2,1},{3,2},{4,3},{5,4},{6,5},{7,6},{9,8},{10,9},{11,10},{12... | collective-permute-start | bytes 196616 | tf_op jit(solution)/shard_map/ppermute | solution.py:19
  46.8 9.0 %collective-permute-start.4 = (bf16[2,2,2,32,1,16,128]{6,3,5,4,2,1,0:T(8,128)(2,1)S(1)}, bf16[2,2,2,32,1,16,128]{6,3,5,4,2,1,0:T(8,128)(2,1)S(1)}, u32[]{:S(2)}, u32[]{:S(2)}) collective-permute-start(bf16[2,2,2,32,1,16,128]{6,3,5,4,2,1,0:T(8,128)(2,1)S(1)} %get-tuple-element.18), channel_id=1, source_target_pairs={{0,8},{8,16},{16,24},{24,32},{32,40},{40,48},{48,56},{56,64},{64,7... | collective-permute-start | bytes 3145736 | tf_op jit(solution)/shard_map/ppermute | solution.py:16
  53.6 5.5 %collective-permute-start.5 = (bf16[2,2,2,32,1,16,128]{6,3,5,4,2,1,0:T(8,128)(2,1)S(1)}, bf16[2,2,2,32,1,16,128]{6,3,5,4,2,1,0:T(8,128)(2,1)S(1)}, u32[]{:S(2)}, u32[]{:S(2)}) collective-permute-start(bf16[2,2,2,32,1,16,128]{6,3,5,4,2,1,0:T(8,128)(2,1)S(1)} %get-tuple-element.19), channel_id=1, source_target_pairs={{8,0},{16,8},{24,16},{32,24},{40,32},{48,40},{56,48},{64,56},{72,6... | collective-permute-start | bytes 3145736 | tf_op jit(solution)/shard_map/ppermute | solution.py:19
  59.1 7.4 %collective-permute-start.6 = (bf16[2,2,2,32,4,1,128]{6,3,5,4,2,1,0:T(8,128)(2,1)S(1)}, bf16[2,2,2,32,4,1,128]{6,3,5,4,2,1,0:T(8,128)(2,1)S(1)}, u32[]{:S(2)}, u32[]{:S(2)}) collective-permute-start(bf16[2,2,2,32,4,1,128]{6,3,5,4,2,1,0:T(8,128)(2,1)S(1)} %get-tuple-element.14), channel_id=1, source_target_pairs={{0,1},{1,2},{2,3},{3,4},{4,5},{5,6},{6,7},{8,9},{9,10},{10,11},{11... | collective-permute-start | bytes 786440 | tf_op jit(solution)/shard_map/ppermute | solution.py:16
  62.7 8.3 %collective-permute-start.7 = (bf16[2,2,2,32,4,1,128]{6,3,5,4,2,1,0:T(8,128)(2,1)S(1)}, bf16[2,2,2,32,4,1,128]{6,3,5,4,2,1,0:T(8,128)(2,1)S(1)}, u32[]{:S(2)}, u32[]{:S(2)}) collective-permute-start(bf16[2,2,2,32,4,1,128]{6,3,5,4,2,1,0:T(8,128)(2,1)S(1)} %get-tuple-element.15), channel_id=1, source_target_pairs={{1,0},{2,1},{3,2},{4,3},{5,4},{6,5},{7,6},{9,8},{10,9},{11,10},{12... | collective-permute-start | bytes 786440 | tf_op jit(solution)/shard_map/ppermute | solution.py:19
  80.9 70.4 %copy-start.1 = (bf16[32,4,18,130]{3,0,2,1:T(8,128)(2,1)}, bf16[32,4,18,130]{3,0,2,1:T(8,128)(2,1)S(1)}, u32[]{:S(2)}) copy-start(bf16[32,4,18,130]{3,0,2,1:T(8,128)(2,1)S(1)} %get-tuple-element.8) | copy-start | bytes 1797124
  80.9 70.7 %copy-start.2 = (bf16[32,4,18,130]{3,0,2,1:T(8,128)(2,1)}, bf16[32,4,18,130]{3,0,2,1:T(8,128)(2,1)S(1)}, u32[]{:S(2)}) copy-start(bf16[32,4,18,130]{3,0,2,1:T(8,128)(2,1)S(1)} %get-tuple-element.9) | copy-start | bytes 1797124
  80.9 74.6 %copy-start.3 = (bf16[32,4,18,130]{3,0,2,1:T(8,128)(2,1)}, bf16[32,4,18,130]{3,0,2,1:T(8,128)(2,1)S(1)}, u32[]{:S(2)}) copy-start(bf16[32,4,18,130]{3,0,2,1:T(8,128)(2,1)S(1)} %get-tuple-element.10) | copy-start | bytes 1797124
  81.0 75.0 %copy-start.4 = (bf16[32,4,18,130]{3,0,2,1:T(8,128)(2,1)}, bf16[32,4,18,130]{3,0,2,1:T(8,128)(2,1)S(1)}, u32[]{:S(2)}) copy-start(bf16[32,4,18,130]{3,0,2,1:T(8,128)(2,1)S(1)} %get-tuple-element.11) | copy-start | bytes 1797124
  81.0 75.9 %copy-start.5 = (bf16[32,4,18,130]{3,0,2,1:T(8,128)(2,1)}, bf16[32,4,18,130]{3,0,2,1:T(8,128)(2,1)S(1)}, u32[]{:S(2)}) copy-start(bf16[32,4,18,130]{3,0,2,1:T(8,128)(2,1)S(1)} %get-tuple-element.6) | copy-start | bytes 1797124
  81.0 76.3 %copy-start.7 = (bf16[32,4,18,130]{3,0,2,1:T(8,128)(2,1)}, bf16[32,4,18,130]{3,0,2,1:T(8,128)(2,1)S(1)}, u32[]{:S(2)}) copy-start(bf16[32,4,18,130]{3,0,2,1:T(8,128)(2,1)S(1)} %get-tuple-element.12) | copy-start | bytes 1797124
  158.6 245.3 %all-reduce.7.cloned.1.call-start = ((), (), s32[]{:S(2)}) async-start(), calls=%async_computation.1 | async-start | bytes 2097152 | tf_op jit(solution)/shard_map/psum | solution.py:125
  178.9 3.3 copy-start.12
  178.9 3.3 copy-start.13
  178.9 3.3 copy-start.14
  178.9 3.3 copy-start.15
  178.9 3.3 copy-start.16
  178.9 3.3 copy-start.17
  (35 other events, 78.4 us)
Sparse Core Ops, SparseCore 0:
  158.8 164.2 all-reduce.4
  325.6 78.3 all-reduce.6
